TPU v7x, 32 devices: a whole 2x2x4 slice. The times are simulated.
32 devices in a mesh: shard: 8 (over y, x, core), rep: 4 (over z).
Axes of the slice: x: 2, y: 2, z: 4, core: 2. Of those that a mesh axis runs over, the one named last changes fastest.
Arguments:
- pooled_grad: float32 [128, 4, 8, 256], P('shard', 'rep'), may hold values from -0.8 to 0.8
- bag_lengths: int32 [8, 4, 128], P('shard', 'rep'), may hold values from 1 to 64, 2048 in all within a row
- row_slots: int32 [8, 4, 2048], P('shard', 'rep'), may hold values from 0 to 511
- id_weights: int32 [8, 4, 2048], P('shard', 'rep'), may hold values from 1 to 32
- touched_rows: float32 [8, 512, 256], P('shard'), may hold values from -6 to 6
- accumulator: float32 [8, 512], P('shard'), may hold values from 0.005 to 0.5
Outputs:
- row_grad: float32 [8, 512, 256], P('shard', 'rep')
- updated_rows: float32 [8, 512, 256], P('shard')
Inputs may be any that keep to these rules, and one draw needn't show every extreme that they name: `bag_lengths`: in each table and replica group the bag lengths sum to 2048.
All inputs are finite; a program needn't handle non-finite values.
Results may differ from a plain program's by a relative error of at most 0.0003.
Values sent between devices are 32-bit elements; how exact they have to be, the bound alone decides.
A program may use at most 64 MiB of HBM per device.

v0:
```python
import jax
import jax.numpy as jnp
from jax import lax
from jax.sharding import PartitionSpec as P

learn_rate = 0.5


def table_rows(arrived, lengths, slots, weights, height):
    ends = jnp.cumsum(lengths)
    starts = ends - lengths
    count = slots.shape[0]
    span = min(512, count)
    turns = count // span
    slot_ids = jnp.arange(height, dtype=jnp.int32)

    def add_block(step, total):
        start = step * span
        positions = start + jnp.arange(span, dtype=jnp.int32)
        target = lax.dynamic_slice_in_dim(slots, start, span)
        factor = lax.dynamic_slice_in_dim(weights, start, span)
        chosen = jnp.where(target[:, None] == slot_ids[None, :], factor[:, None], 0).astype(
            jnp.bfloat16
        )
        member = (
            (positions[:, None] >= starts[None, :]) & (positions[:, None] < ends[None, :])
        ).astype(jnp.bfloat16)
        return total + lax.dot_general(
            chosen, member, (((0,), (0,)), ((), ())), preferred_element_type=jnp.float32
        )

    empty = jnp.zeros((height, arrived.shape[0]), jnp.float32)
    tallies = lax.fori_loop(0, turns, add_block, empty)
    return (
        jnp.dot(
            tallies, arrived, precision=lax.Precision.HIGHEST, preferred_element_type=jnp.float32
        )
        * 0.0625
    )


def adagrad(rows, state, grads):
    new_state = state + jnp.mean(grads * grads, axis=-1)
    return rows - learn_rate * grads / (jnp.sqrt(new_state)[..., None] + 1e-08)


def per_device(pooled_grad, bag_lengths, row_slots, id_weights, touched_rows, accumulator):
    arrived = lax.all_to_all(pooled_grad, "shard", split_axis=2, concat_axis=0, tiled=True)
    height = touched_rows.shape[1]
    owned = touched_rows.shape[0]
    local = jnp.stack(
        [table_rows(arrived[:, 0, 0], bag_lengths[0, 0], row_slots[0, 0], id_weights[0, 0], height)]
    )
    count = height // lax.axis_size("rep")
    start = lax.axis_index("rep") * count
    grad_part = lax.psum_scatter(local, "rep", scatter_dimension=1, tiled=True)
    rows_part = lax.dynamic_slice_in_dim(touched_rows, start, count, 1)
    state_part = lax.dynamic_slice_in_dim(accumulator, start, count, 1)
    fresh = adagrad(rows_part, state_part, grad_part)
    updated = lax.all_gather(fresh, "rep", axis=1, tiled=True)
    return (grad_part, updated)


def solution(mesh):
    placed = (
        P("shard", "rep", None, None),
        P("shard", "rep", None),
        P("shard", "rep", None),
        P("shard", "rep", None),
        P("shard", None, None),
        P("shard", None),
    )
    return jax.shard_map(
        per_device,
        mesh=mesh,
        in_specs=placed,
        out_specs=(P("shard", "rep", None), P("shard", None, None)),
        check_vma=False,
    )
```

profile of v0, /device:TPU:0, one launch (start us, length us, event | category | flops | bytes accessed | tf_op | source)
XLA Modules:
  0.0 74.6 jit_solution(5423783142916893457)
XLA Ops:
  7.2 1.6 %copy.12 = f32[16,1,8,256]{3,0,1,2:T(8,128)} copy(f32[16,1,8,256]{3,2,1,0:T(8,128)} %param.8) | data formatting | bytes 262144 | tf_op args[0]
  8.8 5.2 %all-to-all-start = ((f32[16,1,8,256]{3,0,1,2:T(8,128)}), f32[16,1,8,256]{3,0,1,2:T(8,128)S(1)}, u32[]{:S(2)}, u32[]{:S(2)}) async-start(f32[16,1,8,256]{3,0,1,2:T(8,128)} %copy.12), calls=%async_computation | async-start | bytes 262144 | tf_op jit(solution)/shard_map/all_to_all | solution.py:48
  14.0 0.0 reduce-scatter.2.cloned.1.call-start
  14.0 0.0 copy-start.1
  14.0 0.6 copy-done.1
  14.7 0.1 copy.11
  14.8 0.2 reduce-window.9
  15.0 0.1 reduce.1
  15.1 8.7 %while.14 = (s32[]{:T(128)}, f32[512,128]{1,0:T(8,128)S(1)}, s32[2048]{0:T(1024)}, s32[2048]{0:T(1024)}, s32[128]{0:T(128)S(1)}, /*index=5*/s32[128]{0:T(128)S(1)}, s32[]{:T(128)}, s32[]{:T(128)}, s32[]{:T(128)}, s32[]{:T(128)}) while((s32[]{:T(128)}, f32[512,128]{1,0:T(8,128)S(1)}, s32[2048]{0:T(1024)}, s32[2048]{0:T(1024)}, ...), condition=%wide.region_2.3_spmd.clone, body=%wide.region_1.2_spmd.clone.sunk | while | flops 68223496 | bytes 541873 | solution.py:33
  15.1 0.8 %dynamic_slice.30 = s32[512]{0:T(512)S(1)} dynamic-slice(s32[2048]{0:T(1024)} %get-tuple-element.222, s32[]{:T(128)S(6)} %select_n.28), dynamic_slice_sizes={512} | dynamic-slice | bytes 4100 | tf_op jit(solution)/shard_map/while/body/eval_jaxpr/dynamic_slice | solution.py:21
  15.9 0.8 %dynamic_slice.31 = s32[512]{0:T(512)S(1)} dynamic-slice(s32[2048]{0:T(1024)} %get-tuple-element.221, s32[]{:T(128)S(6)} %select_n.28), dynamic_slice_sizes={512} | dynamic-slice | bytes 4100 | tf_op jit(solution)/shard_map/while/body/eval_jaxpr/dynamic_slice | solution.py:20
  16.6 0.6 convolution_add_fusion.2
  17.3 0.8 %dynamic_slice.30 = s32[512]{0:T(512)S(1)} dynamic-slice(s32[2048]{0:T(1024)} %get-tuple-element.222, s32[]{:T(128)S(6)} %select_n.28), dynamic_slice_sizes={512} | dynamic-slice | bytes 4100 | tf_op jit(solution)/shard_map/while/body/eval_jaxpr/dynamic_slice | solution.py:21
  18.0 0.8 %dynamic_slice.31 = s32[512]{0:T(512)S(1)} dynamic-slice(s32[2048]{0:T(1024)} %get-tuple-element.221, s32[]{:T(128)S(6)} %select_n.28), dynamic_slice_sizes={512} | dynamic-slice | bytes 4100 | tf_op jit(solution)/shard_map/while/body/eval_jaxpr/dynamic_slice | solution.py:20
  18.8 0.6 convolution_add_fusion.2
  19.4 0.8 %dynamic_slice.30 = s32[512]{0:T(512)S(1)} dynamic-slice(s32[2048]{0:T(1024)} %get-tuple-element.222, s32[]{:T(128)S(6)} %select_n.28), dynamic_slice_sizes={512} | dynamic-slice | bytes 4100 | tf_op jit(solution)/shard_map/while/body/eval_jaxpr/dynamic_slice | solution.py:21
  20.2 0.8 %dynamic_slice.31 = s32[512]{0:T(512)S(1)} dynamic-slice(s32[2048]{0:T(1024)} %get-tuple-element.221, s32[]{:T(128)S(6)} %select_n.28), dynamic_slice_sizes={512} | dynamic-slice | bytes 4100 | tf_op jit(solution)/shard_map/while/body/eval_jaxpr/dynamic_slice | solution.py:20
  21.0 0.6 convolution_add_fusion.2
  21.6 0.8 %dynamic_slice.30 = s32[512]{0:T(512)S(1)} dynamic-slice(s32[2048]{0:T(1024)} %get-tuple-element.222, s32[]{:T(128)S(6)} %select_n.28), dynamic_slice_sizes={512} | dynamic-slice | bytes 4100 | tf_op jit(solution)/shard_map/while/body/eval_jaxpr/dynamic_slice | solution.py:21
  22.4 0.8 %dynamic_slice.31 = s32[512]{0:T(512)S(1)} dynamic-slice(s32[2048]{0:T(1024)} %get-tuple-element.221, s32[]{:T(128)S(6)} %select_n.28), dynamic_slice_sizes={512} | dynamic-slice | bytes 4100 | tf_op jit(solution)/shard_map/while/body/eval_jaxpr/dynamic_slice | solution.py:20
  23.1 0.6 convolution_add_fusion.2
  23.8 0.0 all-to-all-done
  23.8 1.4 %fusion.12 = f32[1,512,256]{2,1,0:T(8,128)} fusion(f32[512,128]{1,0:T(8,128)S(1)} %get-tuple-element.126, f32[128,256]{1,0:T(8,128)S(1)} %bitcast.24), kind=kOutput, calls=%fused_computation.16 | convolution fusion | flops 201457664 | bytes 917504 | tf_op jit(solution)/shard_map/dot_general | solution.py:35
  25.1 0.0 reduce-scatter.2.cloned.1.call-update
  25.2 23.7 %reduce-scatter.2.cloned.1.call-done = f32[1,128,256]{2,1,0:T(8,128)} async-done(((f32[1,512,256]{2,1,0:T(8,128)}), f32[1,128,256]{2,1,0:T(8,128)}) %reduce-scatter.2.cloned.1.call-update) | async-done | bytes 131088 | tf_op jit(solution)/shard_map/reduce_scatter | solution.py:56
  48.8 0.0 copy-start
  48.8 1.1 %multiply_reduce_fusion = f32[128]{0:T(128)S(1)} fusion(f32[1,128,256]{2,1,0:T(8,128)} %reduce-scatter.2.cloned.1.call-done), kind=kLoop, calls=%fused_computation.18 | loop fusion | flops 65408 | bytes 131584 | tf_op jit(solution)/shard_map/reduce_sum | solution.py:43
  49.9 0.7 fusion.15
  50.6 0.0 copy-done
  50.6 1.0 %divide_subtract_fusion = f32[1,128,256]{2,1,0:T(8,128)S(1)} fusion(f32[1,128,256]{2,1,0:T(8,128)S(1)} %copy-done, f32[1,512,256]{2,1,0:T(8,128)} %param.12, s32[]{:T(128)S(6)} %select_n.20, f32[128]{0:T(128)S(1)} %fusion.15), kind=kLoop, calls=%fused_computation.17 | loop fusion | flops 98304 | bytes 393732 | tf_op jit(solution)/shard_map/sub | solution.py:44
  51.6 15.3 %all_gather.3 = f32[1,512,256]{2,1,0:T(8,128)S(1)} all-gather(f32[1,128,256]{2,1,0:T(8,128)S(1)} %divide_subtract_fusion), channel_id=1, replica_groups=mesh['shard'=8,'rep'=4] {'rep'}, dimensions={1}, use_global_device_ids=true | all-gather | bytes 655360 | tf_op jit(solution)/shard_map/all_gather | solution.py:60
  66.9 0.8 %copy.20 = f32[1,512,256]{2,1,0:T(8,128)} copy(f32[1,512,256]{2,1,0:T(8,128)S(1)} %all_gather.3) | data formatting | bytes 1048576
  (6 shorter events, 0.0 us)
Async XLA Ops:
  8.8 15.0 %all-to-all-start = ((f32[16,1,8,256]{3,0,1,2:T(8,128)}), f32[16,1,8,256]{3,0,1,2:T(8,128)S(1)}, u32[]{:S(2)}, u32[]{:S(2)}) async-start(f32[16,1,8,256]{3,0,1,2:T(8,128)} %copy.12), calls=%async_computation | async-start | bytes 262144 | tf_op jit(solution)/shard_map/all_to_all | solution.py:48
  14.0 34.9 %reduce-scatter.2.cloned.1.call-start = ((), (), s32[]{:S(2)}) async-start(), calls=%async_computation.2 | async-start | bytes 655360 | tf_op jit(solution)/shard_map/reduce_scatter | solution.py:56
  14.0 0.7 copy-start.1
  48.8 1.8 %copy-start = (f32[1,128,256]{2,1,0:T(8,128)S(1)}, f32[1,128,256]{2,1,0:T(8,128)}, u32[]{:S(2)}) copy-start(f32[1,128,256]{2,1,0:T(8,128)} %reduce-scatter.2.cloned.1.call-done) | copy-start | bytes 393220
Sparse Core Ops, SparseCore 0:
  25.3 23.5 reduce-scatter.1
where the time goes:
time: 75.2 us; the launch traced here: 74.6 us
  waiting for transfers between devices  23.7 us (32%)
  blocking collectives  15.3 us (20%)
  between operations  14.1 us (19%)
  local copies, waits for them, and re-layouts  9.26 us (12%)
  starting transfers between devices  5.23 us (7%)
  matrix products  3.76 us (5%)
  other arithmetic  3.04 us (4%)
    reduce_scatter x1, waiting for transfers between devices, per_device(): grad_part = lax.psum_scatter(local, 'rep', scatter_dimension=1, tiled=True)  23.7 us
    all_gather x1, blocking collectives, per_device(): updated = lax.all_gather(fresh, 'rep', axis=1, tiled=True)  15.3 us
    all_to_all x1, starting transfers between devices, per_device(): lax.all_to_all(pooled_grad, 'shard', split_axis=2, concat_axis=0, tiled=T...  5.2 us
    dynamic_slice x4, local copies, waits for them, and re-layouts, add_block(): factor = lax.dynamic_slice_in_dim(weights, start, span)  3.06 us
    unnamed x6, local copies, waits for them, and re-layouts  3.05 us
    dynamic_slice x4, local copies, waits for them, and re-layouts, add_block(): target = lax.dynamic_slice_in_dim(slots, start, span)  3.04 us
    dot_general x4, matrix products, add_block(): lax.dot_general(chosen, member, (((0,), (0,)), ((), ())), preferred_eleme...  2.4 us
  transfers between devices with their start and end apart: 2, of which 1 were waited for; matrix products, arithmetic and copies ran while one was open for 12% of the time, Pallas kernels for 0%

commit v1 on v0

v1 whole, which is shorter than its diff:
```python
import functools

import jax
import jax.numpy as jnp
from jax import lax
from jax.experimental import pallas as pl
from jax.experimental.pallas import tpu as pltpu
from jax.sharding import PartitionSpec as P

learn_rate = 0.5
MESH = pl.DeviceIdType.MESH


def loop(count, body):
    if count <= 8:
        for i in range(count):
            body(i)
    else:

        @pl.loop(0, count)
        def _(i):
            body(i)


def paired(me, i, count):
    if count & (count - 1):
        return lax.rem(me + i, count)
    out, bit = 0, 1
    while bit < count:
        a = (me // bit) % 2
        b = (i // bit) % 2
        out = out + bit * ((a + b) % 2)
        bit *= 2
    return out


def ring_src(me, i, count):
    if count & (count - 1):
        return lax.rem(me - i + count, count)
    return paired(me, i, count)


def kernel(
    shards, reps, chunks,
    pooled, lengths, slots, weights, touched, state,
    grad_out, rows_out,
    pooled_v, staged, samples, slots_v, weights_v, lengths_v, tally_v, acc, touched_v,
    load_sem, a2a_send, a2a_recv, z_send, z_recv, id_send, id_recv,
):
    me, z = lax.axis_index("shard"), lax.axis_index("rep")
    per = staged.shape[1]
    height, width = acc.shape
    count = samples.shape[1]
    entries = slots_v.shape[2]
    group = shards // chunks
    rows = group * per

    load_pooled = pltpu.make_async_copy(pooled, pooled_v, load_sem.at[0])
    load_touched = pltpu.make_async_copy(touched, touched_v, load_sem.at[1])
    load_pooled.start()
    load_touched.start()

    barrier = pltpu.get_barrier_semaphore()

    def greet(i):
        pl.semaphore_signal(
            barrier, inc=1, device_id={"shard": paired(me, i + 1, shards)}, device_id_type=MESH
        )

    @pl.when(z > 0)
    def _():
        pl.semaphore_signal(barrier, inc=1, device_id={"rep": z - 1}, device_id_type=MESH)

    @pl.when(z < reps - 1)
    def _():
        pl.semaphore_signal(barrier, inc=1, device_id={"rep": z + 1}, device_id_type=MESH)

    loop(shards - 1, greet)

    slots_v[z] = slots[0]
    weights_v[z] = weights[0]
    lengths_v[z] = lengths[0]
    load_pooled.wait()

    def stage(t):
        staged[t] = pooled_v[:, 0, t, :]

    loop(shards, stage)
    samples[z, pl.ds(pl.multiple_of(me * per, per), per), :] = staged[me]

    extra = jnp.where(z > 0, 1, 0) + jnp.where(z < reps - 1, 1, 0)
    pl.semaphore_wait(barrier, shards - 1 + extra)

    sides = ((0, 1), (1, -1))

    def id_copies(g, side, step):
        out = []
        for n, (own, buf) in enumerate(
            ((slots, slots_v), (weights, weights_v), (lengths, lengths_v))
        ):
            out.append(
                pltpu.make_async_remote_copy(
                    src_ref=buf.at[g],
                    dst_ref=buf.at[g],
                    send_sem=id_send.at[side, g, n],
                    recv_sem=id_recv.at[g, n],
                    device_id={"rep": z + step},
                    device_id_type=MESH,
                )
            )
        return out

    def chunk_copy(g, c, side, step):
        part = samples.at[g, pl.ds(pl.multiple_of(c * rows, rows), rows), :]
        return pltpu.make_async_remote_copy(
            src_ref=part,
            dst_ref=part,
            send_sem=z_send.at[side, g, c],
            recv_sem=z_recv.at[g, c],
            device_id={"rep": z + step},
            device_id_type=MESH,
        )

    def has_next(step):
        return (z + step >= 0) & (z + step < reps)

    def a2a_copy(peer, src):
        return pltpu.make_async_remote_copy(
            src_ref=staged.at[peer],
            dst_ref=samples.at[z, pl.ds(pl.multiple_of(src * per, per), per), :],
            send_sem=a2a_send.at[peer],
            recv_sem=a2a_recv.at[src],
            device_id={"shard": peer},
            device_id_type=MESH,
        )

    def send_one(i):
        a2a_copy(paired(me, i + 1, shards), me).start()

    for side, step in sides:

        @pl.when(has_next(step))
        def _(side=side, step=step):
            for copy in id_copies(z, side, step):
                copy.start()

    loop(shards - 1, send_one)

    def tally(g, slot):
        span = min(512, entries)
        lens = lengths_v[g].astype(jnp.float32)
        ii = lax.broadcasted_iota(jnp.int32, (count, count), 0)
        jj = lax.broadcasted_iota(jnp.int32, (count, count), 1)
        ends = jnp.sum(jnp.where(jj <= ii, lens, 0.0), axis=1, keepdims=True).astype(jnp.int32)
        starts = jnp.sum(jnp.where(jj < ii, lens, 0.0), axis=1, keepdims=True).astype(jnp.int32)

        def block(b, total):
            at = pl.multiple_of(b * span, span)
            target = slots_v[g, :, pl.ds(at, span)]
            factor = weights_v[g, :, pl.ds(at, span)].astype(jnp.float32)
            pos = at + lax.broadcasted_iota(jnp.int32, (1, span), 1)
            inside = (pos >= starts) & (pos < ends)
            member = jnp.where(inside, 1.0, 0.0).astype(jnp.bfloat16)
            ids = lax.broadcasted_iota(jnp.int32, (height, span), 0)
            chosen = jnp.where(ids == target, factor, 0.0).astype(jnp.bfloat16)
            return total + lax.dot_general(
                chosen, member, (((1,), (1,)), ((), ())), preferred_element_type=jnp.float32
            )

        total = lax.fori_loop(
            0, entries // span, block, jnp.zeros((height, count), jnp.float32)
        )
        high = total.astype(jnp.bfloat16)
        low = (total - high.astype(jnp.float32)).astype(jnp.bfloat16)
        tally_v[slot, :, :count] = high
        tally_v[slot, :, count:] = low

    def add(g, slot, first=False):
        rest = samples[g]
        total = None
        for _ in range(3):
            part = rest.astype(jnp.bfloat16)
            rest = rest - part.astype(jnp.float32)
            term = jnp.dot(
                tally_v[slot],
                jnp.concatenate([part, part], axis=0),
                preferred_element_type=jnp.float32,
            )
            total = term if total is None else total + term
        if first:
            acc[...] = total
        else:
            acc[...] += total

    tally(z, 0)

    def own_chunk(i):
        c = paired(me // group, i, chunks)

        def arrive(q):
            src = c * group + q

            @pl.when(src != me)
            def _():
                a2a_copy(src, src).wait_recv()

        if group == 1:
            if i > 0:
                a2a_copy(c, c).wait_recv()
        else:
            loop(group, arrive)
        for side, step in sides:

            @pl.when(has_next(step))
            def _(side=side, step=step):
                chunk_copy(z, c, side, step).start()

    for i in range(chunks):
        own_chunk(i)

    add(z, 0, first=True)

    for k in range(1, reps):
        for side, step in sides:
            g = z - k * step

            @pl.when((g >= 0) & (g < reps))
            def _(side=side, step=step, g=g):
                for copy in id_copies(g, side, step):
                    copy.wait_recv()
                if k < reps - 1:

                    @pl.when(has_next(step))
                    def _():
                        for copy in id_copies(g, side, step):
                            copy.start()

        @pl.loop(0, 2)
        def _(side):
            g = z - k * (1 - 2 * side)

            @pl.when((g >= 0) & (g < reps))
            def _():
                tally(g, side)

        for i in range(chunks):
            for side, step in sides:
                g = z - k * step

                @pl.when((g >= 0) & (g < reps))
                def _(side=side, step=step, g=g):
                    c = paired(me // group, i, chunks)
                    chunk_copy(g, c, side, step).wait_recv()
                    if k < reps - 1:

                        @pl.when(has_next(step))
                        def _():
                            chunk_copy(g, c, side, step).start()

        @pl.loop(0, 2)
        def _(side):
            g = z - k * (1 - 2 * side)

            @pl.when((g >= 0) & (g < reps))
            def _():
                add(g, side)

    load_touched.wait()
    acc[...] = acc[...] * 0.0625
    part = height // reps
    grad_out[0] = acc[pl.ds(pl.multiple_of(z * part, part), part), :]
    block = min(128, height)
    ii = lax.broadcasted_iota(jnp.int32, (block, block), 0)
    jj = lax.broadcasted_iota(jnp.int32, (block, block), 1)
    for b in range(height // block):
        at = slice(b * block, (b + 1) * block)
        grads = acc[at, :]
        old = jnp.sum(jnp.where(ii == jj, state[:, at], 0.0), axis=1, keepdims=True)
        new = old + jnp.sum(grads * grads, axis=1, keepdims=True) * (1.0 / width)
        rows_out[0, at, :] = touched_v[0, at, :] - grads * (learn_rate / (jnp.sqrt(new) + 1e-08))

    def sent(i):
        peer = paired(me, i + 1, shards)
        a2a_copy(peer, me).wait_send()

    loop(shards - 1, sent)
    for k in range(reps - 1):
        for side, step in sides:
            g = z - k * step

            @pl.when((g >= 0) & (g < reps) & has_next(step))
            def _(side=side, step=step, g=g):
                for copy in id_copies(g, side, step):
                    copy.wait_send()
                for c in range(chunks):
                    chunk_copy(g, c, side, step).wait_send()


def per_device(pooled_grad, bag_lengths, row_slots, id_weights, touched_rows, accumulator):
    shards, reps = lax.axis_size("shard"), lax.axis_size("rep")
    per, _, tables, width = pooled_grad.shape
    height = touched_rows.shape[1]
    entries = row_slots.shape[2]
    count = per * shards
    chunks = min(8, shards)
    vmem = pl.BlockSpec(memory_space=pltpu.VMEM)
    hbm = pl.BlockSpec(memory_space=pl.ANY)
    dma = pltpu.SemaphoreType.DMA
    return pl.pallas_call(
        functools.partial(kernel, shards, reps, chunks),
        out_shape=(
            jax.ShapeDtypeStruct((1, height // reps, width), jnp.float32),
            jax.ShapeDtypeStruct((1, height, width), jnp.float32),
        ),
        in_specs=[hbm, vmem, vmem, vmem, hbm, vmem],
        out_specs=(vmem, vmem),
        scratch_shapes=[
            pltpu.VMEM((per, 1, tables, width), jnp.float32),
            pltpu.VMEM((tables, per, width), jnp.float32),
            pltpu.VMEM((reps, count, width), jnp.float32),
            pltpu.VMEM((reps, 1, entries), jnp.int32),
            pltpu.VMEM((reps, 1, entries), jnp.int32),
            pltpu.VMEM((reps, 1, count), jnp.int32),
            pltpu.VMEM((2, height, 2 * count), jnp.bfloat16),
            pltpu.VMEM((height, width), jnp.float32),
            pltpu.VMEM((1, height, width), jnp.float32),
            dma((2,)),
            dma((shards,)),
            dma((shards,)),
            dma((2, reps, chunks)),
            dma((reps, chunks)),
            dma((2, reps, 3)),
            dma((reps, 3)),
        ],
        compiler_params=pltpu.CompilerParams(
            collective_id=0, has_side_effects=True, vmem_limit_bytes=60 * 1024 * 1024
        ),
    )(pooled_grad, bag_lengths, row_slots, id_weights, touched_rows, accumulator)


def solution(mesh):
    placed = (
        P("shard", "rep", None, None),
        P("shard", "rep", None),
        P("shard", "rep", None),
        P("shard", "rep", None),
        P("shard", None, None),
        P("shard", None),
    )
    return jax.shard_map(
        per_device,
        mesh=mesh,
        in_specs=placed,
        out_specs=(P("shard", "rep", None), P("shard", None, None)),
        check_vma=False,
    )
```

time: 75.2 us -> 27.6 us (0.37)
  waiting for transfers between devices: 23.7 us -> 0 us
  Pallas kernels: 0 us -> 23.3 us
  blocking collectives: 15.3 us -> 0 us
  between operations: 14.1 us -> 0.64 us
  local copies, waits for them, and re-layouts: 9.26 us -> 3.44 us
  starting transfers between devices: 5.23 us -> 0 us
  matrix products: 3.76 us -> 0 us
  other arithmetic: 3.04 us -> 0 us
    reduce_scatter x1 -> x0, waiting for transfers between devices: 23.7 us -> none  [per_device(): grad_part = lax.psum_scatter(local, 'rep', scatter_dimension=1, tiled=True)]
    pallas_call x0 -> x1, Pallas kernels: none -> 23.3 us  [per_device(): pl.pallas_call(functools.partial(kernel, shards, reps, chunks), out_shape...]
    all_gather x1 -> x0, blocking collectives: 15.3 us -> none  [per_device(): updated = lax.all_gather(fresh, 'rep', axis=1, tiled=True)]
    dynamic_slice x8 -> x0, local copies, waits for them, and re-layouts: 6.1 us -> none  [the longest x4 3.06 us: add_block(): factor = lax.dynamic_slice_in_dim(weights, start, span)]
    all_to_all x1 -> x0, starting transfers between devices: 5.2 us -> none  [per_device(): lax.all_to_all(pooled_grad, 'shard', split_axis=2, concat_axis=0, tiled=T...]
    dot_general x5 -> x0, matrix products: 3.76 us -> none  [the longest x4 2.4 us: add_block(): lax.dot_general(chosen, member, (((0,), (0,)), ((), ())), preferred_eleme...]
    reduce_sum x1 -> x0, other arithmetic: 1.08 us -> none  [adagrad(): new_state = state + jnp.mean(grads * grads, axis=-1)]
    sub x2 -> x0, other arithmetic: 1 us -> none  [the longest x1 1 us: adagrad(): return rows - learn_rate * grads / (jnp.sqrt(new_state)[..., None] + 1e-08)]
  transfers between devices with their start and end apart: 2 -> 0, of which waited for: 1 -> 0; matrix products, arithmetic and copies ran while one was open for 12% -> 0% of each run, Pallas kernels for 0% -> 0%
where the time goes in v1:
time: 27.6 us; the launch traced here: 27.3 us
  Pallas kernels  23.3 us (84%)
  local copies, waits for them, and re-layouts  3.44 us (12%)
  between operations  0.64 us (2%)
    pallas_call x1, Pallas kernels, per_device(): pl.pallas_call(functools.partial(kernel, shards, reps, chunks), out_shape...  23.3 us
    unnamed x2, local copies, waits for them, and re-layouts  3.44 us

profile of v1, /device:TPU:0, one launch (start us, length us, event | category | flops | bytes accessed | tf_op | source)
XLA Modules:
  0.0 27.3 jit_solution(89951095123242155)
XLA Ops:
  0.6 23.3 %shard_map.77 = (f32[1,128,256]{2,1,0:T(8,128)}, f32[1,512,256]{2,1,0:T(8,128)}) custom-call(f32[16,1,8,256]{3,2,1,0:T(8,128)} %pooled.1, s32[1,1,128]{2,1,0:T(1,128)} %lengths.1, s32[1,1,2048]{2,1,0:T(1,128)} %slots.1, s32[1,1,2048]{2,1,0:T(1,128)} %weights.1, f32[1,512,256]{2,1,0:T(8,128)} %touched.1, f32[1,512]{1,0:T(1,128)} %state.1), custom_call_target="tpu_custom_call" | custom-call | tf_op jit(solution)/shard_map/pallas_call | solution.py:309
  23.9 1.6 %copy.10 = f32[1,128,256]{2,1,0:T(8,128)} copy(f32[1,128,256]{2,1,0:T(8,128)} %get-tuple-element.4) | data formatting | bytes 262144
  25.5 1.9 %copy.11 = f32[1,512,256]{2,1,0:T(8,128)} copy(f32[1,512,256]{2,1,0:T(8,128)} %get-tuple-element.5) | data formatting | bytes 1048576

commit v2 on v1

v2 whole, which is shorter than its diff:
```python
import functools

import jax
import jax.numpy as jnp
from jax import lax
from jax.experimental import pallas as pl
from jax.experimental.pallas import tpu as pltpu
from jax.sharding import PartitionSpec as P

learn_rate = 0.5
CHUNKS = 4
REACH = 1
MESH = pl.DeviceIdType.MESH


def loop(count, body):
    if count <= 8:
        for i in range(count):
            body(i)
    else:

        @pl.loop(0, count)
        def _(i):
            body(i)


def paired(me, i, count):
    if count & (count - 1):
        return lax.rem(me + i, count)
    out, bit = 0, 1
    while bit < count:
        a = (me // bit) % 2
        b = (i // bit) % 2
        out = out + bit * ((a + b) % 2)
        bit *= 2
    return out


def ring_src(me, i, count):
    if count & (count - 1):
        return lax.rem(me - i + count, count)
    return paired(me, i, count)


def kernel(
    shards, reps, chunks, reach,
    pooled, lengths, slots, weights,
    acc,
    pooled_v, staged, samples, slots_v, weights_v, lengths_v, tally_v,
    load_sem, a2a_send, a2a_recv, z_send, z_recv, id_send, id_recv,
):
    me, z = lax.axis_index("shard"), lax.axis_index("rep")
    per = staged.shape[1]
    height, width = acc.shape
    count = samples.shape[1]
    entries = slots_v.shape[2]
    group = shards // chunks
    rows = group * per

    load_pooled = pltpu.make_async_copy(pooled, pooled_v, load_sem.at[0])
    load_ids = [
        pltpu.make_async_copy(own.at[0], buf.at[z], load_sem.at[1 + n])
        for n, (own, buf) in enumerate(
            ((slots, slots_v), (weights, weights_v), (lengths, lengths_v))
        )
    ]
    load_pooled.start()
    for copy in load_ids:
        copy.start()

    barrier = pltpu.get_barrier_semaphore()

    def greet(i):
        pl.semaphore_signal(
            barrier, inc=1, device_id={"shard": paired(me, i + 1, shards)}, device_id_type=MESH
        )

    for i in range(1, reps):
        pl.semaphore_signal(
            barrier, inc=1, device_id={"rep": lax.rem(z + i, reps)}, device_id_type=MESH
        )
    loop(shards - 1, greet)

    load_pooled.wait()

    def stage(t):
        staged[t] = pooled_v[:, 0, t, :]

    loop(shards, stage)
    samples[z, pl.ds(pl.multiple_of(me * per, per), per), :] = staged[me]

    pl.semaphore_wait(barrier, shards + reps - 2)

    sides = ((0, 1), (1, -1))

    def id_copies(g, peer):
        out = []
        for n, (own, buf) in enumerate(
            ((slots, slots_v), (weights, weights_v), (lengths, lengths_v))
        ):
            out.append(
                pltpu.make_async_remote_copy(
                    src_ref=own.at[0],
                    dst_ref=buf.at[g],
                    send_sem=id_send.at[peer, n],
                    recv_sem=id_recv.at[g, n],
                    device_id={"rep": peer},
                    device_id_type=MESH,
                )
            )
        return out

    def chunk_copy(g, c, peer):
        part = samples.at[g, pl.ds(pl.multiple_of(c * rows, rows), rows), :]
        return pltpu.make_async_remote_copy(
            src_ref=part,
            dst_ref=part,
            send_sem=z_send.at[peer, g, c],
            recv_sem=z_recv.at[g, c],
            device_id={"rep": peer},
            device_id_type=MESH,
        )

    def inside(at):
        return (at >= 0) & (at < reps)

    def a2a_copy(peer, src):
        return pltpu.make_async_remote_copy(
            src_ref=staged.at[peer],
            dst_ref=samples.at[z, pl.ds(pl.multiple_of(src * per, per), per), :],
            send_sem=a2a_send.at[peer],
            recv_sem=a2a_recv.at[src],
            device_id={"shard": peer},
            device_id_type=MESH,
        )

    def send_one(i):
        a2a_copy(paired(me, i + 1, shards), me).start()

    for i in range(1, reps):
        for copy in id_copies(z, lax.rem(z + i, reps)):
            copy.start()

    loop(shards - 1, send_one)

    def tally(g, slot):
        span = min(512, entries)
        lens = lengths_v[g].astype(jnp.float32)
        ii = lax.broadcasted_iota(jnp.int32, (count, count), 0)
        jj = lax.broadcasted_iota(jnp.int32, (count, count), 1)
        ends = jnp.sum(jnp.where(jj <= ii, lens, 0.0), axis=1, keepdims=True).astype(jnp.int32)
        starts = jnp.sum(jnp.where(jj < ii, lens, 0.0), axis=1, keepdims=True).astype(jnp.int32)

        def block(b, total):
            at = pl.multiple_of(b * span, span)
            target = slots_v[g, :, pl.ds(at, span)]
            factor = weights_v[g, :, pl.ds(at, span)].astype(jnp.float32)
            pos = at + lax.broadcasted_iota(jnp.int32, (1, span), 1)
            within = (pos >= starts) & (pos < ends)
            member = jnp.where(within, 1.0, 0.0).astype(jnp.bfloat16)
            ids = lax.broadcasted_iota(jnp.int32, (height, span), 0)
            chosen = jnp.where(ids == target, factor, 0.0).astype(jnp.bfloat16)
            return total + lax.dot_general(
                chosen, member, (((1,), (1,)), ((), ())), preferred_element_type=jnp.float32
            )

        total = lax.fori_loop(
            0, entries // span, block, jnp.zeros((height, count), jnp.float32)
        )
        high = total.astype(jnp.bfloat16)
        low = (total - high.astype(jnp.float32)).astype(jnp.bfloat16)
        tally_v[slot, :, :count] = high
        tally_v[slot, :, count:] = low

    def add(g, slot, first=False):
        rest = samples[g]
        total = None
        for _ in range(3):
            part = rest.astype(jnp.bfloat16)
            rest = rest - part.astype(jnp.float32)
            term = jnp.dot(
                tally_v[slot],
                jnp.concatenate([part, part], axis=0),
                preferred_element_type=jnp.float32,
            )
            total = term if total is None else total + term
        if first:
            acc[...] = total
        else:
            acc[...] += total

    for copy in load_ids:
        copy.wait()
    tally(z, 0)

    def own_chunk(i):
        c = paired(me // group, i, chunks)

        def arrive(q):
            src = c * group + q

            @pl.when(src != me)
            def _():
                a2a_copy(src, src).wait_recv()

        if group == 1:
            if i > 0:
                a2a_copy(c, c).wait_recv()
        else:
            loop(group, arrive)
        for far in range(1, min(reach, reps - 1) + 1):
            for side, step in sides:
                peer = z + far * step

                @pl.when(inside(peer))
                def _(peer=peer):
                    chunk_copy(z, c, peer).start()

    for i in range(chunks):
        own_chunk(i)

    add(z, 0, first=True)

    for k in range(1, reps):
        for side, step in sides:
            g = z - k * step

            @pl.when(inside(g))
            def _(g=g):
                for copy in id_copies(g, g):
                    copy.wait_recv()

        @pl.loop(0, 2)
        def _(side):
            g = z - k * (1 - 2 * side)

            @pl.when((g >= 0) & (g < reps))
            def _():
                tally(g, side)

        for i in range(chunks):
            for side, step in sides:
                g = z - k * step

                @pl.when(inside(g))
                def _(step=step, g=g):
                    c = paired(me // group, i, chunks)
                    chunk_copy(g, c, g).wait_recv()
                    if reach <= k < reps - 1:

                        @pl.when(inside(z + step))
                        def _():
                            chunk_copy(g, c, z + step).start()

        @pl.loop(0, 2)
        def _(side):
            g = z - k * (1 - 2 * side)

            @pl.when((g >= 0) & (g < reps))
            def _():
                add(g, side)

    acc[...] = acc[...] * 0.0625

    def sent(i):
        peer = paired(me, i + 1, shards)
        a2a_copy(peer, me).wait_send()

    loop(shards - 1, sent)
    for i in range(1, reps):
        for copy in id_copies(z, lax.rem(z + i, reps)):
            copy.wait_send()
    for side, step in sides:
        for far in range(1, min(reach, reps - 1) + 1):
            peer = z + far * step

            @pl.when(inside(peer))
            def _(peer=peer):
                for c in range(chunks):
                    chunk_copy(z, c, peer).wait_send()

        for k in range(reach, reps - 1):
            g = z - k * step

            @pl.when(inside(g) & inside(z + step))
            def _(step=step, g=g):
                for c in range(chunks):
                    chunk_copy(g, c, z + step).wait_send()


def finish(reps, acc, touched, state, grad_out, rows_out):
    z = lax.axis_index("rep")
    height, width = acc.shape
    part = height // reps
    grad_out[0] = acc[pl.ds(pl.multiple_of(z * part, part), part), :]
    block = min(128, height)
    ii = lax.broadcasted_iota(jnp.int32, (block, block), 0)
    jj = lax.broadcasted_iota(jnp.int32, (block, block), 1)
    for b in range(height // block):
        at = slice(b * block, (b + 1) * block)
        grads = acc[at, :]
        old = jnp.sum(jnp.where(ii == jj, state[:, at], 0.0), axis=1, keepdims=True)
        new = old + jnp.sum(grads * grads, axis=1, keepdims=True) * (1.0 / width)
        rows_out[0, at, :] = touched[0, at, :] - grads * (learn_rate / (jnp.sqrt(new) + 1e-08))


def per_device(pooled_grad, bag_lengths, row_slots, id_weights, touched_rows, accumulator):
    shards, reps = lax.axis_size("shard"), lax.axis_size("rep")
    per, _, tables, width = pooled_grad.shape
    height = touched_rows.shape[1]
    entries = row_slots.shape[2]
    count = per * shards
    chunks = min(CHUNKS, shards)
    vmem = pl.BlockSpec(memory_space=pltpu.VMEM)
    hbm = pl.BlockSpec(memory_space=pltpu.HBM)
    dma = pltpu.SemaphoreType.DMA
    sent = [
        pltpu.with_memory_space_constraint(x, pltpu.HBM)
        for x in (pooled_grad, bag_lengths, row_slots, id_weights)
    ]
    total = pl.pallas_call(
        functools.partial(kernel, shards, reps, chunks, REACH),
        out_shape=jax.ShapeDtypeStruct((height, width), jnp.float32),
        in_specs=[hbm] * 4,
        out_specs=vmem,
        scratch_shapes=[
            pltpu.VMEM((per, 1, tables, width), jnp.float32),
            pltpu.VMEM((tables, per, width), jnp.float32),
            pltpu.VMEM((reps, count, width), jnp.float32),
            pltpu.VMEM((reps, 1, entries), jnp.int32),
            pltpu.VMEM((reps, 1, entries), jnp.int32),
            pltpu.VMEM((reps, 1, count), jnp.int32),
            pltpu.VMEM((2, height, 2 * count), jnp.bfloat16),
            dma((4,)),
            dma((shards,)),
            dma((shards,)),
            dma((reps, reps, chunks)),
            dma((reps, chunks)),
            dma((reps, 3)),
            dma((reps, 3)),
        ],
        compiler_params=pltpu.CompilerParams(
            collective_id=0, has_side_effects=True, vmem_limit_bytes=40 * 1024 * 1024
        ),
    )(*sent)
    return pl.pallas_call(
        functools.partial(finish, reps),
        out_shape=(
            jax.ShapeDtypeStruct((1, height // reps, width), jnp.float32),
            jax.ShapeDtypeStruct((1, height, width), jnp.float32),
        ),
        in_specs=[vmem] * 3,
        out_specs=(vmem, vmem),
        compiler_params=pltpu.CompilerParams(vmem_limit_bytes=16 * 1024 * 1024),
    )(total, touched_rows, accumulator)


def solution(mesh):
    placed = (
        P("shard", "rep", None, None),
        P("shard", "rep", None),
        P("shard", "rep", None),
        P("shard", "rep", None),
        P("shard", None, None),
        P("shard", None),
    )
    return jax.shard_map(
        per_device,
        mesh=mesh,
        in_specs=placed,
        out_specs=(P("shard", "rep", None), P("shard", None, None)),
        check_vma=False,
    )
```

time: 27.6 us -> 23.7 us (0.86)
  local copies, waits for them, and re-layouts: 3.44 us -> 0.01 us
  Pallas kernels: 23.3 us -> 22.9 us
    unnamed x2 -> x4, local copies, waits for them, and re-layouts: 3.44 us -> 0.01 us
    pallas_call x1 -> x2, Pallas kernels: 23.3 us -> 22.9 us  [the longest x1 21.8 us: per_device(): pl.pallas_call(functools.partial(kernel, shards, reps, chunks, REACH), ou...]
where the time goes in v2:
time: 23.7 us; the launch traced here: 23.6 us
  Pallas kernels  22.9 us (97%)
  between operations  0.67 us (3%)
    pallas_call x1, Pallas kernels, per_device(): pl.pallas_call(functools.partial(kernel, shards, reps, chunks, REACH), ou...  21.8 us
    pallas_call x1, Pallas kernels, per_device(): pl.pallas_call(functools.partial(finish, reps), out_shape=(jax.ShapeDtype...  1.04 us

profile of v2, /device:TPU:0, one launch (start us, length us, event | category | flops | bytes accessed | tf_op | source)
XLA Modules:
  0.0 23.6 jit_solution(8414230289775563363)
XLA Ops:
  0.6 0.0 copy-start.1
  0.6 0.0 copy-start
  0.7 21.8 %shard_map.77.acc = f32[512,256]{1,0:T(8,128)S(1)} custom-call(f32[16,1,8,256]{3,2,1,0:T(8,128)} %pooled.1, s32[1,1,128]{2,1,0:T(1,128)} %lengths.1, s32[1,1,2048]{2,1,0:T(1,128)} %slots.1, s32[1,1,2048]{2,1,0:T(1,128)} %weights.1), custom_call_target="tpu_custom_call" | custom-call | tf_op jit(solution)/shard_map/pallas_call | solution.py:321
  22.5 0.0 copy-done.1
  22.5 0.0 copy-done
  22.5 1.0 %shard_map.78 = (f32[1,128,256]{2,1,0:T(8,128)}, f32[1,512,256]{2,1,0:T(8,128)}) custom-call(f32[512,256]{1,0:T(8,128)S(1)} %shard_map.77.acc, f32[1,512,256]{2,1,0:T(8,128)S(1)} %copy-done, f32[1,512]{1,0:T(1,128)S(1)} %copy-done.1), custom_call_target="tpu_custom_call" | custom-call | tf_op jit(solution)/shard_map/pallas_call | solution.py:346
Async XLA Ops:
  0.6 21.9 %copy-start.1 = (f32[1,512]{1,0:T(1,128)S(1)}, f32[1,512]{1,0:T(1,128)}, u32[]{:S(2)}) copy-start(f32[1,512]{1,0:T(1,128)} %state.1) | copy-start | bytes 6148
  0.6 21.9 %copy-start = (f32[1,512,256]{2,1,0:T(8,128)S(1)}, f32[1,512,256]{2,1,0:T(8,128)}, u32[]{:S(2)}) copy-start(f32[1,512,256]{2,1,0:T(8,128)} %touched.1) | copy-start | bytes 1572868

commit v3 on v2

--- a/solution.py
+++ b/solution.py
@@ -191,7 +191,7 @@
 
     for copy in load_ids:
         copy.wait()
-    tally(z, 0)
+    tally(z, 2)
 
     def own_chunk(i):
         c = paired(me // group, i, chunks)
@@ -219,8 +219,6 @@
     for i in range(chunks):
         own_chunk(i)
 
-    add(z, 0, first=True)
-
     for k in range(1, reps):
         for side, step in sides:
             g = z - k * step
@@ -251,6 +249,9 @@
                         @pl.when(inside(z + step))
                         def _():
                             chunk_copy(g, c, z + step).start()
+
+        if k == 1:
+            add(z, 2, first=True)
 
         @pl.loop(0, 2)
         def _(side):
@@ -330,7 +331,7 @@
             pltpu.VMEM((reps, 1, entries), jnp.int32),
             pltpu.VMEM((reps, 1, entries), jnp.int32),
             pltpu.VMEM((reps, 1, count), jnp.int32),
-            pltpu.VMEM((2, height, 2 * count), jnp.bfloat16),
+            pltpu.VMEM((3, height, 2 * count), jnp.bfloat16),
             dma((4,)),
             dma((shards,)),
             dma((shards,)),

time: 23.7 us -> 23.3 us (0.983)
  Pallas kernels: 22.9 us -> 22.5 us
    pallas_call x1, Pallas kernels: 21.8 us -> 21.5 us  [per_device(): pl.pallas_call(functools.partial(kernel, shards, reps, chunks, REACH), ou...]
where the time goes in v3:
time: 23.3 us; the launch traced here: 23.2 us
  Pallas kernels  22.5 us (97%)
  between operations  0.67 us (3%)
    pallas_call x1, Pallas kernels, per_device(): pl.pallas_call(functools.partial(kernel, shards, reps, chunks, REACH), ou...  21.5 us
    pallas_call x1, Pallas kernels, per_device(): pl.pallas_call(functools.partial(finish, reps), out_shape=(jax.ShapeDtype...  1.04 us

profile of v3, /device:TPU:0, one launch (start us, length us, event | category | flops | bytes accessed | tf_op | source)
XLA Modules:
  0.0 23.2 jit_solution(18269882358695929541)
XLA Ops:
  0.6 0.0 copy-start.1
  0.6 0.0 copy-start
  0.7 21.5 %shard_map.77.acc = f32[512,256]{1,0:T(8,128)S(1)} custom-call(f32[16,1,8,256]{3,2,1,0:T(8,128)} %pooled.1, s32[1,1,128]{2,1,0:T(1,128)} %lengths.1, s32[1,1,2048]{2,1,0:T(1,128)} %slots.1, s32[1,1,2048]{2,1,0:T(1,128)} %weights.1), custom_call_target="tpu_custom_call" | custom-call | tf_op jit(solution)/shard_map/pallas_call | solution.py:322
  22.1 0.0 copy-done.1
  22.1 0.0 copy-done
  22.1 1.0 %shard_map.78 = (f32[1,128,256]{2,1,0:T(8,128)}, f32[1,512,256]{2,1,0:T(8,128)}) custom-call(f32[512,256]{1,0:T(8,128)S(1)} %shard_map.77.acc, f32[1,512,256]{2,1,0:T(8,128)S(1)} %copy-done, f32[1,512]{1,0:T(1,128)S(1)} %copy-done.1), custom_call_target="tpu_custom_call" | custom-call | tf_op jit(solution)/shard_map/pallas_call | solution.py:347
Async XLA Ops:
  0.6 21.5 %copy-start.1 = (f32[1,512]{1,0:T(1,128)S(1)}, f32[1,512]{1,0:T(1,128)}, u32[]{:S(2)}) copy-start(f32[1,512]{1,0:T(1,128)} %state.1) | copy-start | bytes 6148
  0.6 21.5 %copy-start = (f32[1,512,256]{2,1,0:T(8,128)S(1)}, f32[1,512,256]{2,1,0:T(8,128)}, u32[]{:S(2)}) copy-start(f32[1,512,256]{2,1,0:T(8,128)} %touched.1) | copy-start | bytes 1572868
